TPU v7x, 32 devices: a whole 2x2x4 slice. The times are simulated.
32 devices in a mesh: seq: 8 (over z, core), batch: 4 (over y, x).
Axes of the slice: x: 2, y: 2, z: 4, core: 2. Of those that a mesh axis runs over, the one named last changes fastest.
Arguments:
- tokens: bfloat16 [8, 512, 2048], P('batch', 'seq'), may hold values from -6 to 6
- lengths: int32 [8], P('batch'), may hold values from 256 to 512, as said below
- key_mask: int32 [8, 512], P('batch', 'seq'), may hold values 0 or 1
- top_experts: int32 [8, 512, 4], P('batch', 'seq'), may hold values from 0 to 7, all different within a row
- attn_gain: bfloat16 [2048], P(('seq', 'batch')), may hold values from 0.5 to 2
- query_gain: bfloat16 [2048], P(('seq', 'batch')), may hold values from 0.59765625 to 1.59375
- key_gain: bfloat16 [2048], P(('seq', 'batch')), may hold values from 0.59765625 to 1.59375
- mlp_gain: bfloat16 [2048], P(('seq', 'batch')), may hold values from 0.5 to 2
- w_query: bfloat16 [2048, 2048], P(('seq', 'batch')), may hold values from -0.125 to 0.125
- w_key: bfloat16 [2048, 2048], P(('seq', 'batch')), may hold values from -0.125 to 0.125
- w_value: bfloat16 [2048, 2048], P(('seq', 'batch')), may hold values from -0.125 to 0.125
- w_out: bfloat16 [2048, 2048], P(('seq', 'batch')), may hold values from -1 to 1
- w_router: bfloat16 [2048, 8], P(('seq', 'batch')), may hold values from -0.0625 to 0.0625
- expert_gate: bfloat16 [8, 2048, 1024], P('batch', 'seq'), may hold values from -0.125 to 0.125
- expert_up: bfloat16 [8, 2048, 1024], P('batch', 'seq'), may hold values from -0.125 to 0.125
- expert_down: bfloat16 [8, 1024, 2048], P('batch', 'seq'), may hold values from -1 to 1
- cotangent: bfloat16 [8, 512, 2048], P('batch', 'seq'), may hold values from -6 to 6
Outputs:
- output: bfloat16 [8, 512, 2048], P('batch', 'seq')
- grad_tokens: bfloat16 [8, 512, 2048], P('batch', 'seq')
- grad_attn_gain: float32 [2048], P(('seq', 'batch'))
- grad_query_gain: float32 [2048], P(('seq', 'batch'))
- grad_key_gain: float32 [2048], P(('seq', 'batch'))
- grad_mlp_gain: float32 [2048], P(('seq', 'batch'))
- grad_query: float32 [2048, 2048], P(('seq', 'batch'))
- grad_key: float32 [2048, 2048], P(('seq', 'batch'))
- grad_value: float32 [2048, 2048], P(('seq', 'batch'))
- grad_out: float32 [2048, 2048], P(('seq', 'batch'))
- grad_router: float32 [2048, 8], P(('seq', 'batch'))
- grad_expert_gate: float32 [8, 2048, 1024], P('batch', 'seq')
- grad_expert_up: float32 [8, 2048, 1024], P('batch', 'seq')
- grad_expert_down: float32 [8, 1024, 2048], P('batch', 'seq')
Inputs may be any that keep to these rules, and one draw needn't show every extreme that they name: `lengths`: positions at or past a row's length are padding; some row of every draw is full. `top_experts`: each token names 4 different experts.
All inputs are finite; a program needn't handle non-finite values. No bound on the sum of `key_mask` on one device may be relied on, other than what follows from the above.
Results may differ from a plain program's by a relative error of at most 0.038.
Values may be sent and summed in bfloat16 or wider, within the bound.
A program may use at most 320 MiB of HBM per device.

v0:
```python
import jax
import jax.numpy as jnp
from jax import lax
from jax.sharding import PartitionSpec as P

HEAD = 128
EPS = 1e-05
HIGHEST = lax.Precision.HIGHEST
NEGATIVE = -1e30
BF = jnp.bfloat16
F32 = jnp.float32


def dot(a, b):
    return jnp.dot(a, b, preferred_element_type=F32)


def dot_t(a, b):
    return lax.dot_general(a, b, (((1,), (1,)), ((), ())), preferred_element_type=F32)


def t_dot(a, b):
    return lax.dot_general(a, b, (((0,), (0,)), ((), ())), preferred_element_type=F32)


def rms_scale(v):
    return lax.rsqrt(jnp.mean(v * v, axis=-1, keepdims=True) + EPS)


def rms_back(v, scale, gain, grad):
    normal = v * scale
    weighted = grad * gain
    mean = jnp.mean(weighted * normal, axis=-1, keepdims=True)
    return (scale * (weighted - normal * mean), grad * normal)


def rotary_tables(positions):
    half_head = HEAD // 2
    frequency = 10000.0 ** (-2.0 * jnp.arange(half_head, dtype=F32) / HEAD)
    angles = positions.astype(F32)[:, None] * frequency[None, :]
    return (jnp.cos(angles), jnp.sin(angles))


def rotate(v, cos_part, sin_part):
    first, second = jnp.split(v, 2, axis=-1)
    return jnp.concatenate(
        [first * cos_part - second * sin_part, second * cos_part + first * sin_part], axis=-1
    )


def shards(
    tokens,
    lengths,
    key_mask,
    top_experts,
    attn_gain,
    query_gain,
    key_gain,
    mlp_gain,
    w_query,
    w_key,
    w_value,
    w_out,
    w_router,
    expert_gate,
    expert_up,
    expert_down,
    cotangent,
):
    n_seq = lax.axis_size("seq")
    n_bat = lax.axis_size("batch")
    seq = lax.axis_index("seq")
    bat = lax.axis_index("batch")
    rows, span, dim = tokens.shape
    own = rows * span
    col = n_seq * own
    length = n_seq * span
    shard = w_query.shape[0]
    wide = dim // n_seq
    heads = wide // HEAD
    local_experts, depth, hidden_units = expert_gate.shape
    part = hidden_units // n_seq
    experts = local_experts * n_bat
    every = ("seq", "batch")
    score_scale = HEAD ** (-0.5)
    small = jnp.concatenate(
        [w_router, jnp.stack([attn_gain, query_gain, key_gain, mlp_gain], axis=1)], axis=1
    )
    small_all = lax.all_gather(small, every, axis=0, tiled=True)
    router = small_all[:, :experts]
    gain_attn = small_all[:, experts].astype(F32)
    gain_mlp = small_all[:, experts + 3].astype(F32)
    gain_q = lax.dynamic_slice_in_dim(small_all[:, experts + 1], seq * wide, wide).astype(F32)
    gain_k = lax.dynamic_slice_in_dim(small_all[:, experts + 2], seq * wide, wide).astype(F32)
    qkv_cut = jnp.stack([w_query, w_key, w_value]).reshape(3, shard, n_seq, wide)
    qkv_cut = jnp.transpose(qkv_cut, (2, 1, 0, 3)).reshape(n_seq, shard, 3 * wide)
    qkv_cut = lax.all_to_all(qkv_cut, "seq", 0, 0, tiled=True)
    w_qkv = lax.all_gather(qkv_cut, "batch", axis=1, tiled=True).reshape(dim, 3 * wide)
    w_o = lax.all_gather(w_out, "batch", axis=0, tiled=True)
    gu_cut = jnp.stack([expert_gate, expert_up]).reshape(2, local_experts, depth, n_seq, part)
    gu_cut = jnp.transpose(gu_cut, (3, 2, 0, 1, 4)).reshape(n_seq, depth, 2 * local_experts * part)
    w_gu = lax.all_to_all(gu_cut, "seq", 0, 0, tiled=True).reshape(dim, 2 * local_experts * part)
    w_down = expert_down.reshape(local_experts * part, dim)
    mine = tokens.reshape(own, dim)
    x_col = lax.all_gather(mine, "seq", axis=0, tiled=True).astype(F32)
    scale_x = rms_scale(x_col)
    hidden = (x_col * scale_x * gain_attn).astype(BF)
    qkv = dot(hidden, w_qkv)
    q_pre, k_pre, v_pre = (qkv[:, :wide], qkv[:, wide : 2 * wide], qkv[:, 2 * wide :])
    squares = jnp.stack([jnp.sum(q_pre * q_pre, axis=-1), jnp.sum(k_pre * k_pre, axis=-1)])
    squares = lax.psum(squares, "seq")
    scales = lax.rsqrt(squares / dim + EPS)
    scale_q, scale_k = (scales[0][:, None], scales[1][:, None])

    def by_row(v):
        v = v.reshape(n_seq, rows, span, heads, HEAD)
        return jnp.transpose(v, (1, 3, 0, 2, 4)).reshape(rows, heads, length, HEAD)

    def by_col(v):
        v = v.reshape(rows, heads, n_seq, span, HEAD)
        return jnp.transpose(v, (2, 0, 3, 1, 4)).reshape(col, wide)

    positions = jnp.arange(length, dtype=jnp.int32)
    cos_part, sin_part = rotary_tables(positions)
    q_norm = by_row(q_pre * scale_q)
    k_norm = by_row(k_pre * scale_k)
    gain_qh = gain_q.reshape(1, heads, 1, HEAD)
    gain_kh = gain_k.reshape(1, heads, 1, HEAD)
    queries = rotate(q_norm * gain_qh, cos_part, sin_part).astype(BF)
    keys = rotate(k_norm * gain_kh, cos_part, sin_part).astype(BF)
    values = by_row(v_pre.astype(BF))
    mask_all = lax.all_gather(key_mask, "seq", axis=1, tiled=True)
    usable = (positions[None, :] < lengths[:, None]) & (mask_all == 1)
    causal = positions[None, :] <= positions[:, None]
    same = positions[None, :] == positions[:, None]
    allowed = (causal[None] & (usable[:, None, :] | same[None]))[:, None]
    scores = jnp.einsum("rhqd,rhkd->rhqk", queries, keys, preferred_element_type=F32) * score_scale
    scores = jnp.where(allowed, scores, NEGATIVE)
    top = jnp.max(scores, axis=-1, keepdims=True)
    raised = jnp.exp(scores - top)
    probs = raised / jnp.sum(raised, axis=-1, keepdims=True)
    probs_low = probs.astype(BF)
    attended = jnp.einsum("rhqk,rhkd->rhqd", probs_low, values, preferred_element_type=F32)
    mixed = by_col(attended.astype(BF))
    mixed_out = lax.psum_scatter(dot(mixed, w_o).astype(BF), "seq", scatter_dimension=0, tiled=True)
    x_own = mine.astype(F32)
    residual = x_own + mixed_out.astype(F32)
    scale_r = rms_scale(residual)
    normed = (residual * scale_r * gain_mlp).astype(BF)
    router_probs = jax.nn.softmax(dot(normed, router), axis=-1)
    expert_ids = jnp.arange(experts, dtype=jnp.int32)
    chosen = jnp.any(top_experts.reshape(own, -1)[:, :, None] == expert_ids, axis=1).astype(F32)
    gates = router_probs * chosen
    normed_all = lax.all_gather(normed, every, axis=0, tiled=True)
    gates_all = lax.all_gather(gates, every, axis=0, tiled=True)
    dy_own = cotangent.reshape(own, dim)
    dy_all = lax.all_gather(dy_own, every, axis=0, tiled=True)
    first_expert = bat * local_experts
    gates_here = lax.dynamic_slice_in_dim(gates_all, first_expert, local_experts, 1)
    units = local_experts * part
    gates_wide = jnp.repeat(gates_here, part, axis=1)
    pre = dot(normed_all, w_gu)
    gate_pre, up_pre = (pre[:, :units], pre[:, units:])
    sig = jax.nn.sigmoid(gate_pre)
    silu = gate_pre * sig
    active = (silu * up_pre).astype(BF).astype(F32)
    weighted = (active * gates_wide).astype(BF)
    mixture = dot(weighted, w_down).astype(BF)
    mixture = lax.psum_scatter(mixture, every, scatter_dimension=0, tiled=True)
    output = (residual + mixture.astype(F32)).astype(BF)
    back = dot_t(dy_all, w_down)
    gate_terms = jnp.sum((active * back).reshape(-1, local_experts, part), axis=-1)
    grad_active = back * gates_wide
    grad_gate_pre = (grad_active * up_pre * sig * (1.0 + gate_pre * (1.0 - sig))).astype(BF)
    grad_up_pre = (grad_active * silu).astype(BF)
    grad_pre = jnp.concatenate([grad_gate_pre, grad_up_pre], axis=1)
    grad_down = t_dot(weighted, dy_all)
    grad_gu = t_dot(normed_all, grad_pre).astype(BF)
    grad_normed = dot_t(grad_pre, w_gu).astype(BF)
    grad_normed = lax.psum_scatter(grad_normed, every, scatter_dimension=0, tiled=True).astype(F32)
    grad_gates = lax.dynamic_update_slice_in_dim(
        jnp.zeros((normed_all.shape[0], experts), F32), gate_terms, first_expert, 1
    )
    grad_gates = lax.psum_scatter(grad_gates, every, scatter_dimension=0, tiled=True)
    grad_gu = lax.all_to_all(grad_gu.reshape(n_seq, depth, -1), "seq", 0, 0, tiled=True)
    grad_gu = grad_gu.reshape(n_seq, depth, 2, local_experts, part)
    grad_gu = jnp.transpose(grad_gu, (2, 3, 1, 0, 4)).reshape(2, local_experts, depth, hidden_units)
    grad_gu = grad_gu.astype(F32)
    grad_down = grad_down.reshape(local_experts, part, dim)
    grad_chosen = grad_gates * chosen
    grad_logits = router_probs * (
        grad_chosen - jnp.sum(router_probs * grad_chosen, axis=-1, keepdims=True)
    )
    grad_router = lax.dot_general(
        normed.astype(F32), grad_logits, (((0,), (0,)), ((), ())), precision=HIGHEST
    )
    grad_normed = grad_normed + lax.dot_general(
        grad_logits, router.astype(F32), (((1,), (1,)), ((), ())), precision=HIGHEST
    )
    grad_resid, gain_mlp_terms = rms_back(residual, scale_r, gain_mlp, grad_normed)
    grad_residual = dy_own.astype(F32) + grad_resid
    grad_o = grad_residual.astype(BF)
    grad_o_col = lax.all_gather(grad_o, "seq", axis=0, tiled=True)
    grad_mixed = by_row(dot_t(grad_o_col, w_o).astype(BF))
    grad_w_o = t_dot(mixed, grad_o_col).astype(BF)
    grad_w_o = lax.psum_scatter(grad_w_o, "batch", scatter_dimension=0, tiled=True).astype(F32)
    row_dot = jnp.sum(grad_mixed.astype(F32) * attended, axis=-1, keepdims=True)
    grad_values = jnp.einsum("rhqk,rhqd->rhkd", probs_low, grad_mixed, preferred_element_type=F32)
    grad_probs = jnp.einsum("rhqd,rhkd->rhqk", grad_mixed, values, preferred_element_type=F32)
    grad_scores = (probs * (grad_probs - row_dot)).astype(BF)
    grad_q = score_scale * jnp.einsum(
        "rhqk,rhkd->rhqd", grad_scores, keys, preferred_element_type=F32
    )
    grad_k = score_scale * jnp.einsum(
        "rhqk,rhqd->rhkd", grad_scores, queries, preferred_element_type=F32
    )
    grad_q = rotate(grad_q, cos_part, -sin_part)
    grad_k = rotate(grad_k, cos_part, -sin_part)
    grad_gain_q = jnp.sum(grad_q * q_norm, axis=(0, 2)).reshape(wide)
    grad_gain_k = jnp.sum(grad_k * k_norm, axis=(0, 2)).reshape(wide)
    q_weighted = by_col(grad_q * gain_qh)
    k_weighted = by_col(grad_k * gain_kh)
    q_flat = q_pre * scale_q
    k_flat = k_pre * scale_k
    means = jnp.stack(
        [jnp.sum(q_weighted * q_flat, axis=-1), jnp.sum(k_weighted * k_flat, axis=-1)]
    )
    means = lax.psum(means, "seq") / dim
    grad_q_pre = (scale_q * (q_weighted - q_flat * means[0][:, None])).astype(BF)
    grad_k_pre = (scale_k * (k_weighted - k_flat * means[1][:, None])).astype(BF)
    grad_qkv = jnp.concatenate([grad_q_pre, grad_k_pre, by_col(grad_values).astype(BF)], axis=1)
    grad_hidden = dot_t(grad_qkv, w_qkv).astype(BF)
    grad_hidden = lax.psum_scatter(grad_hidden, "seq", scatter_dimension=0, tiled=True).astype(F32)
    grad_w = t_dot(hidden, grad_qkv).astype(BF).reshape(n_seq, n_bat * shard, 3 * wide)
    grad_w = lax.psum_scatter(grad_w, "batch", scatter_dimension=1, tiled=True)
    grad_w = lax.all_to_all(grad_w, "seq", 0, 0, tiled=True).astype(F32)
    grad_w = grad_w.reshape(n_seq, shard, 3, wide)
    grad_w = jnp.transpose(grad_w, (2, 1, 0, 3)).reshape(3, shard, dim)
    grad_x, gain_attn_terms = rms_back(x_own, rms_scale(x_own), gain_attn, grad_hidden)
    grad_tokens = (grad_residual + grad_x).astype(BF)
    zeros = jnp.zeros((dim,), F32)
    small_grads = jnp.concatenate(
        [
            grad_router,
            jnp.stack(
                [
                    jnp.sum(gain_attn_terms, axis=0),
                    lax.dynamic_update_slice_in_dim(zeros, grad_gain_q, seq * wide, 0),
                    lax.dynamic_update_slice_in_dim(zeros, grad_gain_k, seq * wide, 0),
                    jnp.sum(gain_mlp_terms, axis=0),
                ],
                axis=1,
            ),
        ],
        axis=1,
    )
    small_grads = lax.psum_scatter(small_grads, every, scatter_dimension=0, tiled=True)
    return (
        output.reshape(rows, span, dim),
        grad_tokens.reshape(rows, span, dim),
        small_grads[:, experts],
        small_grads[:, experts + 1],
        small_grads[:, experts + 2],
        small_grads[:, experts + 3],
        grad_w[0],
        grad_w[1],
        grad_w[2],
        grad_w_o,
        small_grads[:, :experts],
        grad_gu[0],
        grad_gu[1],
        grad_down,
    )


def solution(mesh):
    tok = P("batch", "seq", None)
    vec = P(("seq", "batch"))
    mat = P(("seq", "batch"), None)
    in_specs = (tok, P("batch"), P("batch", "seq"), tok) + (vec,) * 4 + (mat,) * 5 + (tok,) * 4
    out_specs = (tok, tok) + (vec,) * 4 + (mat,) * 5 + (tok,) * 3
    return jax.shard_map(shards, mesh=mesh, in_specs=in_specs, out_specs=out_specs, check_vma=False)
```

profile of v0, /device:TPU:0, one launch (start us, length us, event | category | flops | bytes accessed | tf_op | source)
XLA Modules:
  0.0 1895.5 jit_solution(7305523587902170462)
XLA Ops:
  15.1 47.5 %all_to_all.20 = bf16[8,64,768]{2,1,0:T(8,128)(2,1)} all-to-all(bf16[8,64,768]{2,1,0:T(8,128)(2,1)S(1)} %reshape.364), channel_id=1, replica_groups=mesh['seq'=8,'batch'=4] {'seq'}, dimensions={0} | all-to-all | bytes 1572864 | tf_op jit(solution)/shard_map/all_to_all | solution.py:97
  63.6 10.6 all-gather
  74.4 66.6 %all-gather.1 = bf16[32,64,12]{1,2,0:T(8,128)(2,1)S(1)} all-gather(bf16[1,64,12]{1,2,0:T(8,128)(2,1)S(1)} %bitcast.250), channel_id=1, replica_groups=mesh['seq'=8,'batch'=4] {'seq','batch'}, dimensions={0}, use_global_device_ids=true | all-gather | bytes 50688 | tf_op jit(solution)/shard_map/all_gather | solution.py:89
  147.4 6.7 fusion.15
  155.8 14.1 psum.14
  189.9 5.8 fusion.55
  202.2 4.6 convolution_convert_fusion.2
  206.9 46.3 %reduce-scatter.11.cloned.1.call-done = bf16[128,2048]{1,0:T(8,128)(2,1)} async-done(((bf16[1024,2048]{1,0:T(8,128)(2,1)}), bf16[128,2048]{1,0:T(8,128)(2,1)}) %reduce-scatter.11.cloned.1.call-update) | async-done | bytes 524304 | tf_op jit(solution)/shard_map/reduce_scatter | solution.py:145
  270.3 76.5 %all-to-all-done.1 = bf16[8,256,512]{1,2,0:T(8,128)(2,1)} async-done(((bf16[8,256,512]{1,2,0:T(8,128)(2,1)}), bf16[8,256,512]{1,2,0:T(8,128)(2,1)}, u32[]{:S(2)}, u32[]{:S(2)}) %all-to-all-start.1) | async-done | bytes 2097184 | tf_op jit(solution)/shard_map/all_to_all | solution.py:102
  350.7 52.5 %all-gather.15.cloned.1.call-done = bf16[4096,2048]{1,0:T(8,128)(2,1)} async-done(((bf16[128,2048]{1,0:T(8,128)(2,1)}), bf16[4096,2048]{1,0:T(8,128)(2,1)}) %all-gather.15.cloned.1.call-update) | async-done | bytes 16777232 | tf_op jit(solution)/shard_map/all_gather | solution.py:154
  403.2 15.1 fusion.58
  418.3 100.7 %all-gather.17.cloned.1.call-done = bf16[4096,2048]{1,0:T(8,128)(2,1)} async-done(((bf16[128,2048]{1,0:T(8,128)(2,1)}), bf16[4096,2048]{1,0:T(8,128)(2,1)}) %all-gather.17.cloned.1.call-update) | async-done | bytes 16777232 | tf_op jit(solution)/shard_map/all_gather | solution.py:157
  519.0 20.0 %bitcast_reduce_fusion = (f32[4096,2]{0,1:T(2,128)S(1)}, bf16[4096,256]{0,1:T(8,128)(2,1)}, f32[4096,256]{0,1:T(8,128)}) fusion(f32[4096,512]{0,1:T(8,128)} %fusion.58, bf16[4096,2048]{1,0:T(8,128)(2,1)} %all-gather.17.cloned.1.call-done, bf16[256,2048]{1,0:T(8,128)(2,1)S(1)} %bitcast.183), kind=kOutput, calls=%fused_computation.13 | convolution fusion | flops 4304396288 | bytes 32538624 | tf_op jit(solution)/shard_map/dot_general | solution.py:19
  540.8 131.0 %reduce-scatter.17.cloned.1.call-done = f32[128,8]{0,1:T(8,128)} async-done(((f32[4096,8]{0,1:T(8,128)}), f32[128,8]{0,1:T(8,128)}) %reduce-scatter.17.cloned.1.call-update) | async-done | bytes 4112 | tf_op jit(solution)/shard_map/reduce_scatter | solution.py:184
  672.6 64.6 %all_gather.33 = f32[4096,8]{0,1:T(8,128)S(1)} all-gather(f32[128,8]{0,1:T(8,128)S(1)} %get-tuple-element.63), channel_id=1, replica_groups=mesh['seq'=8,'batch'=4] {'seq','batch'}, dimensions={0}, use_global_device_ids=true | all-gather | bytes 135168 | tf_op jit(solution)/shard_map/all_gather | solution.py:155
  737.2 7.3 multiply_convert_fusion.2
  746.6 14.1 convolution_convert_fusion
  760.7 355.7 %reduce-scatter.15.cloned.1.call-done = bf16[128,2048]{1,0:T(8,128)(2,1)} async-done(((bf16[4096,2048]{1,0:T(8,128)(2,1)}), bf16[128,2048]{1,0:T(8,128)(2,1)}) %reduce-scatter.15.cloned.1.call-update) | async-done | bytes 524304 | tf_op jit(solution)/shard_map/reduce_scatter | solution.py:180
  1122.5 48.6 %all-gather.19.cloned.1.call-done = bf16[1024,2048]{1,0:T(8,128)(2,1)} async-done(((bf16[128,2048]{1,0:T(8,128)(2,1)}), bf16[1024,2048]{1,0:T(8,128)(2,1)}) %all-gather.19.cloned.1.call-update) | async-done | bytes 4194320 | tf_op jit(solution)/shard_map/all_gather | solution.py:203
  1171.0 4.6 convolution_convert_fusion.8
  1213.8 14.8 psum.15
  1232.4 5.5 convolution_convert_fusion.4
  1242.6 7.8 convolution_convert_fusion.3
  1250.9 9.9 convolution_convert_fusion.1
  1260.7 14.7 convolution_convert_fusion.5
  1280.1 59.8 %all-to-all-done.3 = bf16[8,256,512]{2,1,0:T(8,128)(2,1)} async-done(((bf16[8,256,512]{2,1,0:T(8,128)(2,1)}), bf16[8,256,512]{2,1,0:T(8,128)(2,1)}, u32[]{:S(2)}, u32[]{:S(2)}) %all-to-all-start.3) | async-done | bytes 2097184 | tf_op jit(solution)/shard_map/all_to_all | solution.py:185
  1343.6 12.4 fusion.59
  1356.2 5.6 reshape.395
  1361.8 4.6 copy.284
  1379.2 4.6 fusion.51
  1390.5 354.9 %reduce-scatter.13.cloned.1.call-done = bf16[128,2048]{1,0:T(8,128)(2,1)} async-done(((bf16[4096,2048]{1,0:T(8,128)(2,1)}), bf16[128,2048]{1,0:T(8,128)(2,1)}) %reduce-scatter.13.cloned.1.call-update) | async-done | bytes 524304 | tf_op jit(solution)/shard_map/reduce_scatter | solution.py:169
  1748.8 135.2 %reduce-scatter.25.cloned.1.call-done = f32[64,12]{1,0:T(8,128)} async-done(((f32[2048,12]{1,0:T(8,128)}), f32[64,12]{1,0:T(8,128)}) %reduce-scatter.25.cloned.1.call-update) | async-done | bytes 3088
  (277 shorter events, 157.7 us)
Async XLA Ops:
  7.2 511.8 %copy-start = (bf16[2,128,2048]{2,1,0:T(8,128)(2,1)S(1)}, bf16[2,128,2048]{2,1,0:T(8,128)(2,1)}, u32[]{:S(2)}) copy-start(bf16[2,128,2048]{2,1,0:T(8,128)(2,1)} %param.32) | copy-start | bytes 3145732
  7.2 137.1 %all-gather.9.cloned.1.call-start = ((), (), s32[]{:S(2)}) async-start(), calls=%async_computation.12 | async-start | bytes 4718592 | tf_op jit(solution)/shard_map/all_gather | solution.py:105
  7.9 139.5 %all-gather.11.cloned.1.call-start = ((), (), s32[]{:S(2)}) async-start(), calls=%async_computation.13 | async-start | bytes 3932160 | tf_op jit(solution)/shard_map/all_gather | solution.py:98
  11.8 51.8 %copy-start.52 = (s32[2,64]{1,0:T(2,128)S(1)}, s32[2,64]{1,0:T(2,128)}, u32[]{:S(2)}) copy-start(s32[2,64]{1,0:T(2,128)} %param.19) | copy-start | bytes 1540
  11.8 62.5 %copy-start.49 = (bf16[64,8]{0,1:T(8,128)(2,1)S(1)}, bf16[64,8]{0,1:T(8,128)(2,1)}, u32[]{:S(2)}) copy-start(bf16[64,8]{0,1:T(8,128)(2,1)} %param.29) | copy-start | bytes 3076
  11.8 62.4 %copy-start.53 = (bf16[64]{0:T(256)(128)(2,1)S(1)}, bf16[64]{0:T(256)(128)(2,1)}, u32[]{:S(2)}) copy-start(bf16[64]{0:T(256)(128)(2,1)} %param.21) | copy-start | bytes 388
  11.9 62.4 %copy-start.54 = (bf16[64]{0:T(256)(128)(2,1)S(1)}, bf16[64]{0:T(256)(128)(2,1)}, u32[]{:S(2)}) copy-start(bf16[64]{0:T(256)(128)(2,1)} %param.22) | copy-start | bytes 388
  11.9 62.4 %copy-start.55 = (bf16[64]{0:T(256)(128)(2,1)S(1)}, bf16[64]{0:T(256)(128)(2,1)}, u32[]{:S(2)}) copy-start(bf16[64]{0:T(256)(128)(2,1)} %param.23) | copy-start | bytes 388
  11.9 62.4 %copy-start.56 = (bf16[64]{0:T(256)(128)(2,1)S(1)}, bf16[64]{0:T(256)(128)(2,1)}, u32[]{:S(2)}) copy-start(bf16[64]{0:T(256)(128)(2,1)} %param.24) | copy-start | bytes 388
  12.3 128.9 %copy-start.57 = (s32[2]{0:T(128)S(1)}, s32[2]{0:T(128)}, u32[]{:S(2)}) copy-start(s32[2]{0:T(128)} %param.18) | copy-start | bytes 28
  62.6 139.6 %all-gather.13.cloned.1.call-start = ((), (), s32[]{:S(2)}) async-start(), calls=%async_computation.14 | async-start | bytes 1310720 | tf_op jit(solution)/shard_map/all_gather | solution.py:99
  63.4 189.8 %reduce-scatter.11.cloned.1.call-start = ((), (), s32[]{:S(2)}) async-start(), calls=%async_computation.15 | async-start | bytes 4718592 | tf_op jit(solution)/shard_map/reduce_scatter | solution.py:145
  206.9 196.3 %all-gather.15.cloned.1.call-start = ((), (), s32[]{:S(2)}) async-start(), calls=%async_computation.16 | async-start | bytes 17301504 | tf_op jit(solution)/shard_map/all_gather | solution.py:154
  256.6 262.4 %all-gather.17.cloned.1.call-start = ((), (), s32[]{:S(2)}) async-start(), calls=%async_computation.18 | async-start | bytes 17301504 | tf_op jit(solution)/shard_map/all_gather | solution.py:157
  265.0 81.8 %all-to-all-start.1 = ((bf16[8,256,512]{1,2,0:T(8,128)(2,1)}), bf16[8,256,512]{1,2,0:T(8,128)(2,1)}, u32[]{:S(2)}, u32[]{:S(2)}) async-start(bf16[8,256,512]{1,2,0:T(8,128)(2,1)} %bitcast.188), calls=%async_computation.2 | async-start | bytes 4194304 | tf_op jit(solution)/shard_map/all_to_all | solution.py:102
  269.4 402.5 %reduce-scatter.17.cloned.1.call-start = ((), (), s32[]{:S(2)}) async-start(), calls=%async_computation.20 | async-start | bytes 135168 | tf_op jit(solution)/shard_map/reduce_scatter | solution.py:184
  539.7 576.7 %reduce-scatter.15.cloned.1.call-start = ((), (), s32[]{:S(2)}) async-start(), calls=%async_computation.19 | async-start | bytes 17301504 | tf_op jit(solution)/shard_map/reduce_scatter | solution.py:180
  672.6 443.9 %copy-start.50 = (f32[128]{0:T(128)}, f32[128]{0:T(128)S(1)}, u32[]{:S(2)}) copy-start(f32[128]{0:T(128)S(1)} %get-tuple-element.62) | copy-start | bytes 1540
  760.6 355.8 %copy-start.31 = (bf16[2048,12]{0,1:T(8,128)(2,1)S(1)}, bf16[2048,12]{0,1:T(8,128)(2,1)}, u32[]{:S(2)}) copy-start(bf16[2048,12]{0,1:T(8,128)(2,1)} %copy-done.30) | copy-start | bytes 147460
  760.7 355.8 %copy-start.36 = (f32[128,8]{0,1:T(8,128)S(1)}, f32[128,8]{0,1:T(8,128)}, u32[]{:S(2)}) copy-start(f32[128,8]{0,1:T(8,128)} %reduce-scatter.17.cloned.1.call-done) | copy-start | bytes 12292
  760.7 355.8 %copy-start.37 = (pred[128,8]{0,1:T(8,128)(4,1)S(1)}, pred[128,8]{0,1:T(8,128)(4,1)}, u32[]{:S(2)}) copy-start(pred[128,8]{0,1:T(8,128)(4,1)} %fusion.33) | copy-start | bytes 3076
  760.7 355.8 %copy-start.45 = (f32[128]{0:T(128)S(1)}, f32[128]{0:T(128)}, u32[]{:S(2)}) copy-start(f32[128]{0:T(128)} %copy-done.44) | copy-start | bytes 1540
  760.7 410.3 %all-gather.19.cloned.1.call-start = ((), (), s32[]{:S(2)}) async-start(), calls=%async_computation.21 | async-start | bytes 4718592 | tf_op jit(solution)/shard_map/all_gather | solution.py:203
  1122.2 217.7 %reduce-scatter.21.cloned.1.call-start = ((), (), s32[]{:S(2)}) async-start(), calls=%async_computation.23 | async-start | bytes 3932160 | tf_op jit(solution)/shard_map/reduce_scatter | solution.py:235
  1237.9 136.4 %reduce-scatter.23.cloned.1.call-start = ((), (), s32[]{:S(2)}) async-start(), calls=%async_computation.24 | async-start | bytes 1310720 | tf_op jit(solution)/shard_map/reduce_scatter | solution.py:206
  1242.5 145.1 %reduce-scatter.19.cloned.1.call-start = ((), (), s32[]{:S(2)}) async-start(), calls=%async_computation.22 | async-start | bytes 4718592 | tf_op jit(solution)/shard_map/reduce_scatter | solution.py:233
  1250.4 495.1 %reduce-scatter.13.cloned.1.call-start = ((), (), s32[]{:S(2)}) async-start(), calls=%async_computation.17 | async-start | bytes 17301504 | tf_op jit(solution)/shard_map/reduce_scatter | solution.py:169
  1275.5 64.4 %all-to-all-start.3 = ((bf16[8,256,512]{2,1,0:T(8,128)(2,1)}), bf16[8,256,512]{2,1,0:T(8,128)(2,1)}, u32[]{:S(2)}, u32[]{:S(2)}) async-start(bf16[8,256,512]{2,1,0:T(8,128)(2,1)} %bitcast.208), calls=%async_computation.10 | async-start | bytes 4194304 | tf_op jit(solution)/shard_map/all_to_all | solution.py:185
  1339.9 37.4 %all-to-all-start.2 = ((bf16[8,64,768]{2,1,0:T(8,128)(2,1)}), bf16[8,64,768]{2,1,0:T(8,128)(2,1)S(1)}, u32[]{:S(2)}, u32[]{:S(2)}) async-start(bf16[8,64,768]{2,1,0:T(8,128)(2,1)} %reduce-scatter.21.cloned.1.call-done), calls=%async_computation.8 | async-start | bytes 1572864 | tf_op jit(solution)/shard_map/all_to_all | solution.py:236
  1343.5 540.5 %reduce-scatter.25.cloned.1.call-start = ((), (), s32[]{:S(2)}) async-start(), calls=%async_computation.25 | async-start | bytes 1081344
  1384.1 361.4 %copy-start.6 = (bf16[128,2048]{1,0:T(8,128)(2,1)S(1)}, bf16[128,2048]{1,0:T(8,128)(2,1)}, u32[]{:S(2)}) copy-start(bf16[128,2048]{1,0:T(8,128)(2,1)} %reduce-scatter.11.cloned.1.call-done) | copy-start | bytes 1572868
  1384.1 361.4 %copy-start.8 = (bf16[2,64,2048]{2,1,0:T(8,128)(2,1)S(1)}, bf16[2,64,2048]{2,1,0:T(8,128)(2,1)}, u32[]{:S(2)}) copy-start(bf16[2,64,2048]{2,1,0:T(8,128)(2,1)} %param.33) | copy-start | bytes 1572868
  (43 other events, 409.9 us)
Sparse Core Ops, SparseCore 0:
  9.6 66.5 all-gather.8
  78.1 43.6 all-gather.10
  123.6 26.6 all-gather.12
  207.0 46.1 reduce-scatter.10
  256.7 146.4 all-gather.14
  405.9 113.0 all-gather.16
  539.9 131.9 reduce-scatter.16
  760.8 355.6 reduce-scatter.14
  1122.4 48.6 all-gather.18
  1238.0 42.0 reduce-scatter.20
  1283.3 27.7 reduce-scatter.22
  1313.2 66.1 reduce-scatter.18
  1381.7 363.7 reduce-scatter.12
  1747.6 136.3 reduce-scatter.24
where the time goes:
time: 1900 us
  waiting for transfers between devices  1360 us (72%)
  blocking collectives  218 us (11%)
  matrix products  138 us (7%)
  local copies, waits for them, and re-layouts  89.4 us (5%)
  other arithmetic  56.6 us (3%)
    reduce_scatter x1, waiting for transfers between devices, shards(): lax.psum_scatter(grad_normed, every, scatter_dimension=0, tiled=True)  356 us
    reduce_scatter x1, waiting for transfers between devices, shards(): mixture = lax.psum_scatter(mixture, every, scatter_dimension=0, tiled=True)  355 us
    unnamed x15, waiting for transfers between devices  137 us
    reduce_scatter x1, waiting for transfers between devices, shards(): lax.psum_scatter(grad_gates, every, scatter_dimension=0, tiled=True)  131 us
    all_gather x1, waiting for transfers between devices, shards(): dy_all = lax.all_gather(dy_own, every, axis=0, tiled=True)  101 us
    all_to_all x1, waiting for transfers between devices, shards(): lax.all_to_all(gu_cut, 'seq', 0, 0, tiled=True)  76.5 us
    all_gather x1, blocking collectives, shards(): small_all = lax.all_gather(small, every, axis=0, tiled=True)  66.6 us
    all_gather x1, blocking collectives, shards(): gates_all = lax.all_gather(gates, every, axis=0, tiled=True)  64.6 us
  transfers between devices with their start and end apart: 17, of which 11 were waited for; matrix products, arithmetic and copies ran while one was open for 9% of the time, Pallas kernels for 0%

commit v1 on v0

--- a/solution.py
+++ b/solution.py
@@ -200,7 +200,15 @@
     grad_resid, gain_mlp_terms = rms_back(residual, scale_r, gain_mlp, grad_normed)
     grad_residual = dy_own.astype(F32) + grad_resid
     grad_o = grad_residual.astype(BF)
-    grad_o_col = lax.all_gather(grad_o, "seq", axis=0, tiled=True)
+    ways, here = (lax.axis_size("seq"), lax.axis_index("seq"))
+    grown, reach = (grad_o, 1)
+    while reach < ways:
+        theirs = lax.ppermute(grown, "seq", [(d, d ^ reach) for d in range(ways)])
+        mine_first = jnp.concatenate([grown, theirs], axis=0)
+        theirs_first = jnp.concatenate([theirs, grown], axis=0)
+        grown = jnp.where(here & reach == 0, mine_first, theirs_first)
+        reach = 2 * reach
+    grad_o_col = grown
     grad_mixed = by_row(dot_t(grad_o_col, w_o).astype(BF))
     grad_w_o = t_dot(mixed, grad_o_col).astype(BF)
     grad_w_o = lax.psum_scatter(grad_w_o, "batch", scatter_dimension=0, tiled=True).astype(F32)

time: 1900 us -> 1990 us (1.047)
  waiting for transfers between devices: 1360 us -> 1430 us
    ppermute x0 -> x3, waiting for transfers between devices: none -> 117 us  [shards(): theirs = lax.ppermute(grown, 'seq', [(d, d ^ reach) for d in range(ways)])]
    all_gather x1 -> x0, waiting for transfers between devices: 48.6 us -> none  [shards(): grad_o_col = lax.all_gather(grad_o, 'seq', axis=0, tiled=True)]
    unnamed x15 -> x14, waiting for transfers between devices: 137 us -> 137 us
  transfers between devices with their start and end apart: 17 -> 19, of which waited for: 11 -> 12; matrix products, arithmetic and copies ran while one was open for 9% -> 8% of each run, Pallas kernels for 0% -> 0%
where the time goes in v1:
time: 1990 us; the launch traced here: 1980 us
  waiting for transfers between devices  1430 us (72%)
  blocking collectives  220 us (11%)
  matrix products  141 us (7%)
  local copies, waits for them, and re-layouts  89.3 us (4%)
  other arithmetic  63.9 us (3%)
    reduce_scatter x1, waiting for transfers between devices, shards(): lax.psum_scatter(grad_normed, every, scatter_dimension=0, tiled=True)  355 us
    reduce_scatter x1, waiting for transfers between devices, shards(): mixture = lax.psum_scatter(mixture, every, scatter_dimension=0, tiled=True)  353 us
    unnamed x14, waiting for transfers between devices  137 us
    reduce_scatter x1, waiting for transfers between devices, shards(): lax.psum_scatter(grad_gates, every, scatter_dimension=0, tiled=True)  131 us
    ppermute x3, waiting for transfers between devices, shards(): theirs = lax.ppermute(grown, 'seq', [(d, d ^ reach) for d in range(ways)])  117 us
    all_gather x1, waiting for transfers between devices, shards(): dy_all = lax.all_gather(dy_own, every, axis=0, tiled=True)  101 us
    all_to_all x1, waiting for transfers between devices, shards(): lax.all_to_all(gu_cut, 'seq', 0, 0, tiled=True)  76.5 us
    all_gather x1, blocking collectives, shards(): small_all = lax.all_gather(small, every, axis=0, tiled=True)  66.6 us
  transfers between devices with their start and end apart: 19, of which 12 were waited for; matrix products, arithmetic and copies ran while one was open for 8% of the time, Pallas kernels for 0%

profile of v1, /device:TPU:0, one launch (start us, length us, event | category | flops | bytes accessed | tf_op | source)
XLA Modules:
  0.0 1979.0 jit_solution(6593629117438228304)
XLA Ops:
  15.1 47.5 %all_to_all.20 = bf16[8,64,768]{2,1,0:T(8,128)(2,1)} all-to-all(bf16[8,64,768]{2,1,0:T(8,128)(2,1)S(1)} %reshape.364), channel_id=1, replica_groups=mesh['seq'=8,'batch'=4] {'seq'}, dimensions={0} | all-to-all | bytes 1572864 | tf_op jit(solution)/shard_map/all_to_all | solution.py:97
  63.6 10.6 all-gather
  74.4 66.6 %all-gather.1 = bf16[32,64,12]{1,2,0:T(8,128)(2,1)S(1)} all-gather(bf16[1,64,12]{1,2,0:T(8,128)(2,1)S(1)} %bitcast.248), channel_id=1, replica_groups=mesh['seq'=8,'batch'=4] {'seq','batch'}, dimensions={0}, use_global_device_ids=true | all-gather | bytes 50688 | tf_op jit(solution)/shard_map/all_gather | solution.py:89
  147.4 6.7 fusion.15
  155.8 14.4 psum.14
  190.1 5.8 fusion.57
  207.2 46.3 %reduce-scatter.11.cloned.1.call-done = bf16[128,2048]{1,0:T(8,128)(2,1)} async-done(((bf16[1024,2048]{1,0:T(8,128)(2,1)}), bf16[128,2048]{1,0:T(8,128)(2,1)}) %reduce-scatter.11.cloned.1.call-update) | async-done | bytes 524304 | tf_op jit(solution)/shard_map/reduce_scatter | solution.py:145
  270.6 76.5 %all-to-all-done.1 = bf16[8,256,512]{1,2,0:T(8,128)(2,1)} async-done(((bf16[8,256,512]{1,2,0:T(8,128)(2,1)}), bf16[8,256,512]{1,2,0:T(8,128)(2,1)}, u32[]{:S(2)}, u32[]{:S(2)}) %all-to-all-start.1) | async-done | bytes 2097184 | tf_op jit(solution)/shard_map/all_to_all | solution.py:102
  351.0 52.5 %all-gather.14.cloned.1.call-done = bf16[4096,2048]{1,0:T(8,128)(2,1)} async-done(((bf16[128,2048]{1,0:T(8,128)(2,1)}), bf16[4096,2048]{1,0:T(8,128)(2,1)}) %all-gather.14.cloned.1.call-update) | async-done | bytes 16777232 | tf_op jit(solution)/shard_map/all_gather | solution.py:154
  403.5 15.1 fusion.60
  418.6 100.7 %all-gather.16.cloned.1.call-done = bf16[4096,2048]{1,0:T(8,128)(2,1)} async-done(((bf16[128,2048]{1,0:T(8,128)(2,1)}), bf16[4096,2048]{1,0:T(8,128)(2,1)}) %all-gather.16.cloned.1.call-update) | async-done | bytes 16777232 | tf_op jit(solution)/shard_map/all_gather | solution.py:157
  519.3 20.0 %bitcast_reduce_fusion = (f32[4096,2]{0,1:T(2,128)S(1)}, bf16[4096,256]{0,1:T(8,128)(2,1)}, f32[4096,256]{0,1:T(8,128)}) fusion(f32[4096,512]{0,1:T(8,128)} %fusion.60, bf16[4096,2048]{1,0:T(8,128)(2,1)} %all-gather.16.cloned.1.call-done, bf16[256,2048]{1,0:T(8,128)(2,1)S(1)} %bitcast.181), kind=kOutput, calls=%fused_computation.14 | convolution fusion | flops 4304396288 | bytes 32538624 | tf_op jit(solution)/shard_map/dot_general | solution.py:19
  541.1 131.0 %reduce-scatter.17.cloned.1.call-done = f32[128,8]{0,1:T(8,128)} async-done(((f32[4096,8]{0,1:T(8,128)}), f32[128,8]{0,1:T(8,128)}) %reduce-scatter.17.cloned.1.call-update) | async-done | bytes 4112 | tf_op jit(solution)/shard_map/reduce_scatter | solution.py:184
  672.9 64.2 %all_gather.30 = f32[4096,8]{0,1:T(8,128)S(1)} all-gather(f32[128,8]{0,1:T(8,128)S(1)} %get-tuple-element.63), channel_id=1, replica_groups=mesh['seq'=8,'batch'=4] {'seq','batch'}, dimensions={0}, use_global_device_ids=true | all-gather | bytes 135168 | tf_op jit(solution)/shard_map/all_gather | solution.py:155
  737.1 7.3 multiply_convert_fusion.2
  746.4 14.1 convolution_convert_fusion
  761.0 355.3 %reduce-scatter.15.cloned.1.call-done = bf16[128,2048]{1,0:T(8,128)(2,1)} async-done(((bf16[4096,2048]{1,0:T(8,128)(2,1)}), bf16[128,2048]{1,0:T(8,128)(2,1)}) %reduce-scatter.15.cloned.1.call-update) | async-done | bytes 524304 | tf_op jit(solution)/shard_map/reduce_scatter | solution.py:180
  1129.0 23.8 %collective-permute-done.1 = bf16[256,2048]{1,0:T(8,128)(2,1)} collective-permute-done((bf16[256,2048]{1,0:T(8,128)(2,1)}, bf16[256,2048]{1,0:T(8,128)(2,1)}, u32[]{:S(2)}, u32[]{:S(2)}) %collective-permute-start.1) | collective-permute-done | bytes 1048608 | tf_op jit(solution)/shard_map/ppermute | solution.py:206
  1160.3 90.7 %collective-permute-done.2 = bf16[512,2048]{1,0:T(8,128)(2,1)} collective-permute-done((bf16[512,2048]{1,0:T(8,128)(2,1)}, bf16[512,2048]{1,0:T(8,128)(2,1)}, u32[]{:S(2)}, u32[]{:S(2)}) %collective-permute-start.2) | collective-permute-done | bytes 2097184 | tf_op jit(solution)/shard_map/ppermute | solution.py:206
  1251.0 5.9 convolution_convert_fusion.8
  1295.1 16.9 psum.15
  1315.7 5.5 convolution_convert_fusion.4
  1321.4 5.9 convolution_convert_fusion.6
  1327.5 7.7 convolution_convert_fusion.3
  1335.3 9.9 convolution_convert_fusion.1
  1345.3 14.7 convolution_convert_fusion.5
  1364.6 62.0 %all-to-all-done.3 = bf16[8,256,512]{2,1,0:T(8,128)(2,1)} async-done(((bf16[8,256,512]{2,1,0:T(8,128)(2,1)}), bf16[8,256,512]{2,1,0:T(8,128)(2,1)}, u32[]{:S(2)}, u32[]{:S(2)}) %all-to-all-start.3) | async-done | bytes 2097184 | tf_op jit(solution)/shard_map/all_to_all | solution.py:185
  1430.5 12.4 fusion.61
  1443.2 5.4 reshape.395
  1448.7 4.7 copy.284
  1476.1 352.6 %reduce-scatter.13.cloned.1.call-done = bf16[128,2048]{1,0:T(8,128)(2,1)} async-done(((bf16[4096,2048]{1,0:T(8,128)(2,1)}), bf16[128,2048]{1,0:T(8,128)(2,1)}) %reduce-scatter.13.cloned.1.call-update) | async-done | bytes 524304 | tf_op jit(solution)/shard_map/reduce_scatter | solution.py:169
  1832.0 135.2 %reduce-scatter.25.cloned.1.call-done = f32[64,12]{1,0:T(8,128)} async-done(((f32[2048,12]{1,0:T(8,128)}), f32[64,12]{1,0:T(8,128)}) %reduce-scatter.25.cloned.1.call-update) | async-done | bytes 3088
  (282 shorter events, 175.7 us)
Async XLA Ops:
  7.2 512.1 %copy-start = (bf16[2,128,2048]{2,1,0:T(8,128)(2,1)S(1)}, bf16[2,128,2048]{2,1,0:T(8,128)(2,1)}, u32[]{:S(2)}) copy-start(bf16[2,128,2048]{2,1,0:T(8,128)(2,1)} %param.32) | copy-start | bytes 3145732
  7.2 137.1 %all-gather.8.cloned.1.call-start = ((), (), s32[]{:S(2)}) async-start(), calls=%async_computation.12 | async-start | bytes 4718592 | tf_op jit(solution)/shard_map/all_gather | solution.py:105
  7.9 139.5 %all-gather.10.cloned.1.call-start = ((), (), s32[]{:S(2)}) async-start(), calls=%async_computation.13 | async-start | bytes 3932160 | tf_op jit(solution)/shard_map/all_gather | solution.py:98
  11.8 62.5 %copy-start.49 = (bf16[64,8]{0,1:T(8,128)(2,1)S(1)}, bf16[64,8]{0,1:T(8,128)(2,1)}, u32[]{:S(2)}) copy-start(bf16[64,8]{0,1:T(8,128)(2,1)} %param.29) | copy-start | bytes 3076
  11.8 62.4 %copy-start.53 = (bf16[64]{0:T(256)(128)(2,1)S(1)}, bf16[64]{0:T(256)(128)(2,1)}, u32[]{:S(2)}) copy-start(bf16[64]{0:T(256)(128)(2,1)} %param.21) | copy-start | bytes 388
  11.9 62.4 %copy-start.54 = (bf16[64]{0:T(256)(128)(2,1)S(1)}, bf16[64]{0:T(256)(128)(2,1)}, u32[]{:S(2)}) copy-start(bf16[64]{0:T(256)(128)(2,1)} %param.22) | copy-start | bytes 388
  11.9 62.4 %copy-start.55 = (bf16[64]{0:T(256)(128)(2,1)S(1)}, bf16[64]{0:T(256)(128)(2,1)}, u32[]{:S(2)}) copy-start(bf16[64]{0:T(256)(128)(2,1)} %param.23) | copy-start | bytes 388
  12.3 128.9 %copy-start.57 = (s32[2]{0:T(128)S(1)}, s32[2]{0:T(128)}, u32[]{:S(2)}) copy-start(s32[2]{0:T(128)} %param.18) | copy-start | bytes 28
  62.6 139.9 %all-gather.12.cloned.1.call-start = ((), (), s32[]{:S(2)}) async-start(), calls=%async_computation.14 | async-start | bytes 1310720 | tf_op jit(solution)/shard_map/all_gather | solution.py:99
  63.4 190.1 %reduce-scatter.11.cloned.1.call-start = ((), (), s32[]{:S(2)}) async-start(), calls=%async_computation.15 | async-start | bytes 4718592 | tf_op jit(solution)/shard_map/reduce_scatter | solution.py:145
  207.2 196.3 %all-gather.14.cloned.1.call-start = ((), (), s32[]{:S(2)}) async-start(), calls=%async_computation.16 | async-start | bytes 17301504 | tf_op jit(solution)/shard_map/all_gather | solution.py:154
  256.9 262.4 %all-gather.16.cloned.1.call-start = ((), (), s32[]{:S(2)}) async-start(), calls=%async_computation.18 | async-start | bytes 17301504 | tf_op jit(solution)/shard_map/all_gather | solution.py:157
  265.3 81.8 %all-to-all-start.1 = ((bf16[8,256,512]{1,2,0:T(8,128)(2,1)}), bf16[8,256,512]{1,2,0:T(8,128)(2,1)}, u32[]{:S(2)}, u32[]{:S(2)}) async-start(bf16[8,256,512]{1,2,0:T(8,128)(2,1)} %bitcast.186), calls=%async_computation.2 | async-start | bytes 4194304 | tf_op jit(solution)/shard_map/all_to_all | solution.py:102
  269.7 402.5 %reduce-scatter.17.cloned.1.call-start = ((), (), s32[]{:S(2)}) async-start(), calls=%async_computation.20 | async-start | bytes 135168 | tf_op jit(solution)/shard_map/reduce_scatter | solution.py:184
  540.0 576.3 %reduce-scatter.15.cloned.1.call-start = ((), (), s32[]{:S(2)}) async-start(), calls=%async_computation.19 | async-start | bytes 17301504 | tf_op jit(solution)/shard_map/reduce_scatter | solution.py:180
  672.9 443.5 %copy-start.50 = (f32[128]{0:T(128)}, f32[128]{0:T(128)S(1)}, u32[]{:S(2)}) copy-start(f32[128]{0:T(128)S(1)} %get-tuple-element.62) | copy-start | bytes 1540
  760.5 355.8 %copy-start.31 = (bf16[2048,12]{0,1:T(8,128)(2,1)S(1)}, bf16[2048,12]{0,1:T(8,128)(2,1)}, u32[]{:S(2)}) copy-start(bf16[2048,12]{0,1:T(8,128)(2,1)} %copy-done.30) | copy-start | bytes 147460
  760.5 355.8 %copy-start.36 = (f32[128,8]{0,1:T(8,128)S(1)}, f32[128,8]{0,1:T(8,128)}, u32[]{:S(2)}) copy-start(f32[128,8]{0,1:T(8,128)} %reduce-scatter.17.cloned.1.call-done) | copy-start | bytes 12292
  760.5 355.8 %copy-start.37 = (pred[128,8]{0,1:T(8,128)(4,1)S(1)}, pred[128,8]{0,1:T(8,128)(4,1)}, u32[]{:S(2)}) copy-start(pred[128,8]{0,1:T(8,128)(4,1)} %fusion.33) | copy-start | bytes 3076
  760.5 355.8 %copy-start.45 = (f32[128]{0:T(128)S(1)}, f32[128]{0:T(128)}, u32[]{:S(2)}) copy-start(f32[128]{0:T(128)} %copy-done.44) | copy-start | bytes 1540
  760.5 666.1 %reduce-scatter.21.cloned.1.call-start = ((), (), s32[]{:S(2)}) async-start(), calls=%async_computation.22 | async-start | bytes 3932160 | tf_op jit(solution)/shard_map/reduce_scatter | solution.py:243
  1122.1 2.3 collective-permute-start
  1127.3 25.5 %collective-permute-start.1 = (bf16[256,2048]{1,0:T(8,128)(2,1)}, bf16[256,2048]{1,0:T(8,128)(2,1)}, u32[]{:S(2)}, u32[]{:S(2)}) collective-permute-start(bf16[256,2048]{1,0:T(8,128)(2,1)} %maximum_select_fusion.2), channel_id=1, source_target_pairs={{0,8},{4,12},{8,0},{12,4},{16,24},{20,28},{24,16},{28,20},{1,9},{5... | collective-permute-start | bytes 3145736 | tf_op jit(solution)/shard_map/ppermute | solution.py:206
  1157.3 93.7 %collective-permute-start.2 = (bf16[512,2048]{1,0:T(8,128)(2,1)}, bf16[512,2048]{1,0:T(8,128)(2,1)}, u32[]{:S(2)}, u32[]{:S(2)}) collective-permute-start(bf16[512,2048]{1,0:T(8,128)(2,1)} %maximum_select_fusion.1), channel_id=1, source_target_pairs={{0,16},{4,20},{8,24},{12,28},{16,0},{20,4},{24,8},{28,12},{1,17},{... | collective-permute-start | bytes 6291464 | tf_op jit(solution)/shard_map/ppermute | solution.py:206
  1321.3 139.8 %reduce-scatter.23.cloned.1.call-start = ((), (), s32[]{:S(2)}) async-start(), calls=%async_computation.23 | async-start | bytes 1310720 | tf_op jit(solution)/shard_map/reduce_scatter | solution.py:214
  1327.3 145.9 %reduce-scatter.19.cloned.1.call-start = ((), (), s32[]{:S(2)}) async-start(), calls=%async_computation.21 | async-start | bytes 4718592 | tf_op jit(solution)/shard_map/reduce_scatter | solution.py:241
  1335.3 493.4 %reduce-scatter.13.cloned.1.call-start = ((), (), s32[]{:S(2)}) async-start(), calls=%async_computation.17 | async-start | bytes 17301504 | tf_op jit(solution)/shard_map/reduce_scatter | solution.py:169
  1360.0 66.6 %all-to-all-start.3 = ((bf16[8,256,512]{2,1,0:T(8,128)(2,1)}), bf16[8,256,512]{2,1,0:T(8,128)(2,1)}, u32[]{:S(2)}, u32[]{:S(2)}) async-start(bf16[8,256,512]{2,1,0:T(8,128)(2,1)} %bitcast.206), calls=%async_computation.10 | async-start | bytes 4194304 | tf_op jit(solution)/shard_map/all_to_all | solution.py:185
  1426.6 36.3 %all-to-all-start.2 = ((bf16[8,64,768]{2,1,0:T(8,128)(2,1)}), bf16[8,64,768]{2,1,0:T(8,128)(2,1)S(1)}, u32[]{:S(2)}, u32[]{:S(2)}) async-start(bf16[8,64,768]{2,1,0:T(8,128)(2,1)} %reduce-scatter.21.cloned.1.call-done), calls=%async_computation.8 | async-start | bytes 1572864 | tf_op jit(solution)/shard_map/all_to_all | solution.py:244
  1430.2 537.1 %reduce-scatter.25.cloned.1.call-start = ((), (), s32[]{:S(2)}) async-start(), calls=%async_computation.24 | async-start | bytes 1081344
  1469.7 359.0 %copy-start.6 = (bf16[128,2048]{1,0:T(8,128)(2,1)S(1)}, bf16[128,2048]{1,0:T(8,128)(2,1)}, u32[]{:S(2)}) copy-start(bf16[128,2048]{1,0:T(8,128)(2,1)} %reduce-scatter.11.cloned.1.call-done) | copy-start | bytes 1572868
  1469.7 359.0 %copy-start.8 = (bf16[2,64,2048]{2,1,0:T(8,128)(2,1)S(1)}, bf16[2,64,2048]{2,1,0:T(8,128)(2,1)}, u32[]{:S(2)}) copy-start(bf16[2,64,2048]{2,1,0:T(8,128)(2,1)} %param.33) | copy-start | bytes 1572868
  (45 other events, 532.8 us)
Sparse Core Ops, SparseCore 0:
  9.6 66.5 all-gather.7
  78.1 43.6 all-gather.9
  123.6 26.6 all-gather.11
  207.3 46.1 reduce-scatter.10
  257.0 146.4 all-gather.13
  406.2 113.0 all-gather.15
  540.1 131.9 reduce-scatter.16
  760.7 355.6 reduce-scatter.14
  1321.4 41.6 reduce-scatter.20
  1366.1 27.7 reduce-scatter.22
  1396.2 66.1 reduce-scatter.18
  1464.5 364.1 reduce-scatter.12
  1830.9 136.2 reduce-scatter.24
